TPU v7x, 256 devices: a whole 4x4x8 slice. The times are simulated.
256 devices in a mesh: space: 64 (over x, z, core), mode: 4 (over y).
Axes of the slice: x: 4, y: 4, z: 8, core: 2. Of those that a mesh axis runs over, the one named last changes fastest.
Arguments:
- modes_in: bfloat16 [120, 131072], P('mode', 'space'), may hold values from -6 to 6
- blocks: bfloat16 [5, 4608, 128, 128], P(None, 'space'), may hold values from -0.25 to 0.25
- block_cols: int32 [1152, 4], P('space'), may hold values from 0 to 15
- send_slot: int32 [16384], P('space'), may hold values from 0 to 511, as said below
- recv_row: int32 [32768], P('space'), may hold values from 0 to 2048, as said below
- mix_cols: int32 [5, 120, 8], replicated, may hold values from 0 to 120, as said below
- mix_coef: float32 [5, 120, 8], replicated, as said below
Outputs:
- first_apply: bfloat16 [120, 131072], P('mode', 'space')
- second_apply: bfloat16 [120, 131072], P('mode', 'space')
Inputs may be any that keep to these rules, and one draw needn't show every extreme that they name: Interface row e of subdomain d goes to subdomain send_slot[d * 256 + e] // 8 at position send_slot[d * 256 + e] % 8. A subdomain's entries are distinct, and for each destination they fill positions from 0 upward, at most 8; one destination, the same for all subdomains, gets 8 rows from every subdomain. `recv_row`: entry o * 64 * 8 + d * 8 + p is the own degree of freedom of subdomain o at which position p from subdomain d is added; it is 2048 exactly where subdomain d sends fewer than p + 1 rows to o. Live entries may repeat. `mix_cols`: column 120 marks a padded slot. Each row of each term has from 4 to 8 live slots, both reached; live columns may repeat. `mix_coef`: zero exactly on padded slots.
All inputs are finite; a program needn't handle non-finite values.
Results may differ from a plain program's by a relative error of at most 0.022.
Values may be sent and summed in bfloat16 or wider, within the bound.
No kernel may reach another device: no remote copies, remote signals or barrier semaphores. Data moves between devices by JAX's collectives and lax.ppermute only.
A program may use at most 64 MiB of HBM per device.

v0:
```python
import jax
import jax.numpy as jnp
from jax import lax
from jax.sharding import PartitionSpec as P


def dense_mixer(mix_cols, mix_coef):
    mode_count = mix_coef.shape[1]
    columns = jnp.arange(mode_count, dtype=jnp.int32)
    onehot_table = (mix_cols[..., None] == columns).astype(jnp.float32)
    return jnp.sum(mix_coef[..., None] * onehot_table, axis=2).astype(jnp.bfloat16)


def block_rows(field_blocks, stiffness, block_cols):
    picked = field_blocks[:, :, block_cols, :]
    return jnp.einsum("mkcnd,kcnde->mce", picked, stiffness, preferred_element_type=jnp.float32)


def local(modes_in, blocks, block_cols, send_slot, recv_row, mix_cols, mix_coef):
    chaos_mixer = dense_mixer(mix_cols, mix_coef)
    term_count = blocks.shape[0]
    block_size = blocks.shape[-1]
    out_blocks, stored = block_cols.shape
    stiffness = blocks.reshape(term_count, out_blocks, stored, block_size, block_size)
    modes_dev, owned_dofs = modes_in.shape
    owned_blocks = owned_dofs // block_size
    slot_total = recv_row.shape[0]

    def send_partials(partials):
        flat_rows = partials.reshape(modes_dev, -1)
        packed = jnp.zeros((modes_dev, slot_total), jnp.float32).at[:, send_slot].set(flat_rows)
        return lax.all_to_all(
            packed.astype(jnp.bfloat16), "space", split_axis=1, concat_axis=1, tiled=True
        ).astype(packed.dtype)

    def mix_field(field_now):
        regrouped = lax.all_to_all(field_now, "mode", split_axis=1, concat_axis=0, tiled=True)
        mixed_all = jnp.einsum(
            "kij,jn->ikn", chaos_mixer, regrouped, preferred_element_type=jnp.float32
        ).astype(jnp.bfloat16)
        return lax.all_to_all(mixed_all, "mode", split_axis=0, concat_axis=2, tiled=True)

    def one_apply(field_now):
        mixed_field = mix_field(field_now)
        field_blocks = mixed_field.reshape(modes_dev, term_count, owned_blocks, block_size)
        products = block_rows(field_blocks, stiffness, block_cols)
        arrived = send_partials(products[:, owned_blocks:])
        owned_part = products[:, :owned_blocks]
        owned_flat = owned_part.reshape(modes_dev, owned_dofs)
        summed = owned_flat.at[:, recv_row].add(arrived, mode="drop")
        return summed.astype(jnp.bfloat16)

    first_apply = one_apply(modes_in)
    second_apply = one_apply(first_apply)
    return (first_apply, second_apply)


def solution(mesh):
    in_specs = (
        P("mode", "space"),
        P(None, "space", None, None),
        P("space", None),
        P("space"),
        P("space"),
        P(),
        P(),
    )
    out_specs = (P("mode", "space"), P("mode", "space"))
    return jax.shard_map(local, mesh=mesh, in_specs=in_specs, out_specs=out_specs, check_vma=False)
```

profile of v0, /device:TPU:1, one launch (start us, length us, event | category | flops | bytes accessed | tf_op | source)
XLA Modules:
  0.0 132.8 jit_solution(6629927610011276790)
XLA Ops:
  0.6 1.0 all_to_all.62
  2.3 5.0 %all-to-all-start = ((bf16[30,4,512]{2,0,1:T(8,128)(2,1)}), bf16[30,4,512]{2,0,1:T(8,128)(2,1)S(1)}, u32[]{:S(2)}, u32[]{:S(2)}) async-start(bf16[30,4,512]{2,0,1:T(8,128)(2,1)} %copy.74), calls=%async_computation | async-start | bytes 262144 | tf_op jit(solution)/shard_map/all_to_all | solution.py:37
  9.1 3.5 %select_reduce_fusion = bf16[5,120,120]{2,1,0:T(8,128)(2,1)S(1)} fusion(f32[5,120,8]{2,1,0:T(8,128)S(1)} %copy.73, s32[5,120,8]{2,1,0:T(8,128)S(1)} %copy.72), kind=kLoop, calls=%fused_computation.12 | loop fusion | flops 1656000 | bytes 182400 | tf_op jit(solution)/shard_map/reduce_sum | solution.py:11
  13.0 1.2 copy.75
  14.1 4.2 %all-to-all-start.1 = ((bf16[120,5,512]{2,1,0:T(8,128)(2,1)}), bf16[120,5,512]{2,1,0:T(8,128)(2,1)S(1)}, u32[]{:S(2)}, u32[]{:S(2)}) async-start(bf16[120,5,512]{2,1,0:T(8,128)(2,1)} %copy.75), calls=%async_computation.1 | async-start | bytes 1966080 | tf_op jit(solution)/shard_map/all_to_all | solution.py:41
  18.6 12.1 %all-to-all-done.1 = bf16[120,5,512]{2,1,0:T(8,128)(2,1)S(1)} async-done(((bf16[120,5,512]{2,1,0:T(8,128)(2,1)}), bf16[120,5,512]{2,1,0:T(8,128)(2,1)S(1)}, u32[]{:S(2)}, u32[]{:S(2)}) %all-to-all-start.1) | async-done | bytes 614432 | tf_op jit(solution)/shard_map/all_to_all | solution.py:41
  31.7 2.7 %gather_fusion = bf16[72,30,5,128]{3,1,2,0:T(8,128)(2,1)} fusion(bf16[30,5,16,128]{3,0,2,1:T(8,128)(2,1)S(1)} %copy.79, s32[1024]{0:T(1024)S(1)} %pad_clamp_fusion), kind=kCustom, calls=%fused_computation | custom fusion | bytes 5529888 | tf_op jit(solution)/shard_map/gather | solution.py:15
  34.4 2.9 %copy.80 = bf16[72,30,5,128]{3,0,2,1:T(8,128)(2,1)S(1)} copy(bf16[72,30,5,128]{3,1,2,0:T(8,128)(2,1)} %gather_fusion) | data formatting | bytes 5529600 | tf_op jit(solution)/shard_map/gather | solution.py:15
  37.3 5.4 %fusion.8 = f32[30,18,128]{2,0,1:T(8,128)S(1)} fusion(bf16[5,18,4,128,128]{4,3,2,1,0:T(8,128)(2,1)} %bitcast.85, bf16[30,5,18,4,128]{4,3,2,1,0:T(4,128)(2,1)S(1)} %bitcast.77), kind=kOutput, calls=%fused_computation.18 | convolution fusion | flops 353894400 | bytes 14837760 | tf_op jit(solution)/shard_map/mkcnd,kcnde->mce/dot_general | solution.py:16
  43.0 1.2 scatter_custom_fusion
  44.9 14.5 %all-to-all-start.2 = ((bf16[30,64,8]{0,2,1:T(8,128)(2,1)}), bf16[30,64,8]{0,2,1:T(8,128)(2,1)S(1)}, u32[]{:S(2)}, u32[]{:S(2)}) async-start(bf16[30,64,8]{0,2,1:T(8,128)(2,1)} %convert_bitcast_fusion.5), calls=%async_computation.2 | async-start | bytes 262144 | tf_op jit(solution)/shard_map/all_to_all | solution.py:32
  59.8 10.0 %all-to-all-done.2 = bf16[30,64,8]{0,2,1:T(8,128)(2,1)S(1)} async-done(((bf16[30,64,8]{0,2,1:T(8,128)(2,1)}), bf16[30,64,8]{0,2,1:T(8,128)(2,1)S(1)}, u32[]{:S(2)}, u32[]{:S(2)}) %all-to-all-start.2) | async-done | bytes 30752 | tf_op jit(solution)/shard_map/all_to_all | solution.py:32
  69.7 3.7 %scatter_custom_fusion.1 = f32[30,2048]{0,1:T(8,128)S(1)} fusion(f32[30,2048]{0,1:T(8,128)S(1)} %bitcast.74, s32[512]{0:T(512)S(1)} %compare_select_fusion, bf16[30,64,8]{0,2,1:T(8,128)(2,1)S(1)} %all-to-all-done.2), kind=kCustom, calls=%fused_computation.23 | custom fusion | flops 30720 | bytes 376832 | tf_op jit(solution)/shard_map/scatter-add | solution.py:50
  73.7 7.2 %all_to_all.86 = bf16[30,4,512]{2,0,1:T(8,128)(2,1)S(1)} all-to-all(bf16[30,4,512]{2,0,1:T(8,128)(2,1)S(1)} %copy.87), channel_id=1, replica_groups=mesh['space'=64,'mode'=4] {'mode'}, dimensions={1} | all-to-all | bytes 245760 | tf_op jit(solution)/shard_map/all_to_all | solution.py:37
  81.5 15.3 %all_to_all.87 = bf16[120,5,512]{2,1,0:T(8,128)(2,1)S(1)} all-to-all(bf16[120,5,512]{2,1,0:T(8,128)(2,1)S(1)} %copy.88), channel_id=1, replica_groups=mesh['space'=64,'mode'=4] {'mode'}, dimensions={0} | all-to-all | bytes 1228800 | tf_op jit(solution)/shard_map/all_to_all | solution.py:41
  97.8 2.7 %gather_fusion.1 = bf16[72,30,5,128]{3,1,2,0:T(8,128)(2,1)} fusion(bf16[30,5,16,128]{3,0,2,1:T(8,128)(2,1)S(1)} %copy.91, s32[1024]{0:T(1024)S(1)} %pad_clamp_fusion), kind=kCustom, calls=%fused_computation.1 | custom fusion | bytes 5529888 | tf_op jit(solution)/shard_map/gather | solution.py:15
  100.5 2.9 %copy.92 = bf16[72,30,5,128]{3,0,2,1:T(8,128)(2,1)S(1)} copy(bf16[72,30,5,128]{3,1,2,0:T(8,128)(2,1)} %gather_fusion.1) | data formatting | bytes 5529600 | tf_op jit(solution)/shard_map/gather | solution.py:15
  103.4 5.4 %fusion.13 = f32[30,18,128]{2,0,1:T(8,128)S(1)} fusion(bf16[5,18,4,128,128]{4,3,2,1,0:T(8,128)(2,1)} %bitcast.86, bf16[30,5,18,4,128]{4,3,2,1,0:T(4,128)(2,1)S(1)} %bitcast.78), kind=kOutput, calls=%fused_computation.19 | convolution fusion | flops 353894400 | bytes 14837760 | tf_op jit(solution)/shard_map/mkcnd,kcnde->mce/dot_general | solution.py:16
  109.0 1.2 scatter_custom_fusion.2
  110.9 6.8 %all-to-all-start.5 = ((bf16[30,64,8]{0,2,1:T(8,128)(2,1)}), bf16[30,64,8]{0,2,1:T(8,128)(2,1)S(1)}, u32[]{:S(2)}, u32[]{:S(2)}) async-start(bf16[30,64,8]{0,2,1:T(8,128)(2,1)} %convert_bitcast_fusion.4), calls=%async_computation.5 | async-start | bytes 262144 | tf_op jit(solution)/shard_map/all_to_all | solution.py:32
  117.8 0.9 copy.99
  119.1 9.1 %all-to-all-done.5 = bf16[30,64,8]{0,2,1:T(8,128)(2,1)S(1)} async-done(((bf16[30,64,8]{0,2,1:T(8,128)(2,1)}), bf16[30,64,8]{0,2,1:T(8,128)(2,1)S(1)}, u32[]{:S(2)}, u32[]{:S(2)}) %all-to-all-start.5) | async-done | bytes 30752 | tf_op jit(solution)/shard_map/all_to_all | solution.py:32
  128.1 3.7 %scatter_custom_fusion.3 = f32[30,2048]{0,1:T(8,128)S(1)} fusion(f32[30,2048]{0,1:T(8,128)S(1)} %bitcast.73, s32[512]{0:T(512)S(1)} %compare_select_fusion, bf16[30,64,8]{0,2,1:T(8,128)(2,1)S(1)} %all-to-all-done.5), kind=kCustom, calls=%fused_computation.21 | custom fusion | flops 30720 | bytes 376832 | tf_op jit(solution)/shard_map/scatter-add | solution.py:50
  131.9 0.9 copy.100
  (46 shorter events, 8.2 us)
Async XLA Ops:
  2.3 10.3 %all-to-all-start = ((bf16[30,4,512]{2,0,1:T(8,128)(2,1)}), bf16[30,4,512]{2,0,1:T(8,128)(2,1)S(1)}, u32[]{:S(2)}, u32[]{:S(2)}) async-start(bf16[30,4,512]{2,0,1:T(8,128)(2,1)} %copy.74), calls=%async_computation | async-start | bytes 262144 | tf_op jit(solution)/shard_map/all_to_all | solution.py:37
  8.2 10.2 %copy-start = (s32[18,4]{0,1:T(4,128)S(1)}, s32[18,4]{0,1:T(4,128)}, u32[]{:S(2)}) copy-start(s32[18,4]{0,1:T(4,128)} %param.9) | copy-start | bytes 868
  8.2 10.4 %copy-start.2 = (s32[256]{0:T(256)S(1)}, s32[256]{0:T(256)}, u32[]{:S(2)}) copy-start(s32[256]{0:T(256)} %param.10) | copy-start | bytes 3076
  14.1 16.6 %all-to-all-start.1 = ((bf16[120,5,512]{2,1,0:T(8,128)(2,1)}), bf16[120,5,512]{2,1,0:T(8,128)(2,1)S(1)}, u32[]{:S(2)}, u32[]{:S(2)}) async-start(bf16[120,5,512]{2,1,0:T(8,128)(2,1)} %copy.75), calls=%async_computation.1 | async-start | bytes 1966080 | tf_op jit(solution)/shard_map/all_to_all | solution.py:41
  37.3 22.0 %copy-start.1 = (s32[512]{0:T(512)S(1)}, s32[512]{0:T(512)}, u32[]{:S(2)}) copy-start(s32[512]{0:T(512)} %param.11) | copy-start | bytes 6148
  44.9 24.9 %all-to-all-start.2 = ((bf16[30,64,8]{0,2,1:T(8,128)(2,1)}), bf16[30,64,8]{0,2,1:T(8,128)(2,1)S(1)}, u32[]{:S(2)}, u32[]{:S(2)}) async-start(bf16[30,64,8]{0,2,1:T(8,128)(2,1)} %convert_bitcast_fusion.5), calls=%async_computation.2 | async-start | bytes 262144 | tf_op jit(solution)/shard_map/all_to_all | solution.py:32
  110.9 17.2 %all-to-all-start.5 = ((bf16[30,64,8]{0,2,1:T(8,128)(2,1)}), bf16[30,64,8]{0,2,1:T(8,128)(2,1)S(1)}, u32[]{:S(2)}, u32[]{:S(2)}) async-start(bf16[30,64,8]{0,2,1:T(8,128)(2,1)} %convert_bitcast_fusion.4), calls=%async_computation.5 | async-start | bytes 262144 | tf_op jit(solution)/shard_map/all_to_all | solution.py:32
where the time goes:
time: 133 us
  waiting for transfers between devices  31.1 us (23%)
  starting transfers between devices  30.6 us (23%)
  local copies, waits for them, and re-layouts  23.9 us (18%)
  blocking collectives  22.5 us (17%)
  other arithmetic  12.3 us (9%)
  matrix products  11.4 us (9%)
    all_to_all x2, starting transfers between devices, send_partials(): lax.all_to_all(packed.astype(jnp.bfloat16), 'space', split_axis=1, concat...  21.3 us
    all_to_all x2, waiting for transfers between devices, send_partials(): lax.all_to_all(packed.astype(jnp.bfloat16), 'space', split_axis=1, concat...  19 us
    all_to_all x1, blocking collectives, mix_field(): lax.all_to_all(mixed_all, 'mode', split_axis=0, concat_axis=2, tiled=True)  15.3 us
    all_to_all x1, waiting for transfers between devices, mix_field(): lax.all_to_all(mixed_all, 'mode', split_axis=0, concat_axis=2, tiled=True)  12.1 us
    gather x4, local copies, waits for them, and re-layouts, block_rows(): picked = field_blocks[:, :, block_cols, :]  11.3 us
    dot_general x2, matrix products, block_rows(): jnp.einsum('mkcnd,kcnde->mce', picked, stiffness, preferred_element_type=...  10.8 us
    scatter-add x2, other arithmetic, one_apply(): summed = owned_flat.at[:, recv_row].add(arrived, mode='drop')  7.39 us
    all_to_all x1, blocking collectives, mix_field(): lax.all_to_all(field_now, 'mode', split_axis=1, concat_axis=0, tiled=True)  7.22 us
  transfers between devices with their start and end apart: 4, of which 3 were waited for; matrix products, arithmetic and copies ran while one was open for 5% of the time, Pallas kernels for 0%

commit v1 on v0

--- a/solution.py
+++ b/solution.py
@@ -38,7 +38,12 @@
         mixed_all = jnp.einsum(
             "kij,jn->ikn", chaos_mixer, regrouped, preferred_element_type=jnp.float32
         ).astype(jnp.bfloat16)
-        return lax.all_to_all(mixed_all, "mode", split_axis=0, concat_axis=2, tiled=True)
+        return jnp.concatenate(
+            lax.all_to_all(
+                jnp.stack(jnp.split(mixed_all, lax.axis_size("mode"), axis=0)), "mode", 0, 0
+            ),
+            axis=2,
+        )
 
     def one_apply(field_now):
         mixed_field = mix_field(field_now)

time: 133 us -> 126 us (0.947)
  waiting for transfers between devices: 31.1 us -> 27.3 us
  blocking collectives: 22.5 us -> 18.9 us
    all_to_all x1, waiting for transfers between devices: 12.1 us -> 8.3 us  [mix_field(): lax.all_to_all(jnp.stack(jnp.split(mixed_all, lax.axis_size('mode'), axis...]
    all_to_all x1, blocking collectives: 15.3 us -> 11.7 us  [mix_field(): lax.all_to_all(jnp.stack(jnp.split(mixed_all, lax.axis_size('mode'), axis...]
    convert_element_type x2 -> x0, local copies, waits for them, and re-layouts: 1.42 us -> none  [mix_field(): mixed_all = jnp.einsum('kij,jn->ikn', chaos_mixer, regrouped, preferred_e...]
  transfers between devices with their start and end apart: 4 -> 4, of which waited for: 3 -> 3; matrix products, arithmetic and copies ran while one was open for 5% -> 6% of each run, Pallas kernels for 0% -> 0%
where the time goes in v1:
time: 126 us
  starting transfers between devices  31 us (25%)
  waiting for transfers between devices  27.3 us (22%)
  local copies, waits for them, and re-layouts  22.6 us (18%)
  blocking collectives  18.9 us (15%)
  other arithmetic  13.4 us (11%)
  matrix products  11.4 us (9%)
    all_to_all x2, starting transfers between devices, send_partials(): lax.all_to_all(packed.astype(jnp.bfloat16), 'space', split_axis=1, concat...  21.7 us
    all_to_all x2, waiting for transfers between devices, send_partials(): lax.all_to_all(packed.astype(jnp.bfloat16), 'space', split_axis=1, concat...  19 us
    all_to_all x1, blocking collectives, mix_field(): lax.all_to_all(jnp.stack(jnp.split(mixed_all, lax.axis_size('mode'), axis...  11.7 us
    gather x4, local copies, waits for them, and re-layouts, block_rows(): picked = field_blocks[:, :, block_cols, :]  11.3 us
    dot_general x2, matrix products, block_rows(): jnp.einsum('mkcnd,kcnde->mce', picked, stiffness, preferred_element_type=...  10.8 us
    all_to_all x1, waiting for transfers between devices, mix_field(): lax.all_to_all(jnp.stack(jnp.split(mixed_all, lax.axis_size('mode'), axis...  8.3 us
    scatter-add x2, other arithmetic, one_apply(): summed = owned_flat.at[:, recv_row].add(arrived, mode='drop')  7.39 us
    all_to_all x1, blocking collectives, mix_field(): lax.all_to_all(field_now, 'mode', split_axis=1, concat_axis=0, tiled=True)  7.22 us
  transfers between devices with their start and end apart: 4, of which 3 were waited for; matrix products, arithmetic and copies ran while one was open for 6% of the time, Pallas kernels for 0%

profile of v1, /device:TPU:1, one launch (start us, length us, event | category | flops | bytes accessed | tf_op | source)
XLA Modules:
  0.0 125.6 jit_solution(15763148590981107466)
XLA Ops:
  0.6 1.0 all_to_all.46
  2.3 5.0 %all-to-all-start = ((bf16[30,4,512]{2,0,1:T(8,128)(2,1)}), bf16[30,4,512]{2,0,1:T(8,128)(2,1)S(1)}, u32[]{:S(2)}, u32[]{:S(2)}) async-start(bf16[30,4,512]{2,0,1:T(8,128)(2,1)} %copy.45), calls=%async_computation | async-start | bytes 262144 | tf_op jit(solution)/shard_map/all_to_all | solution.py:37
  9.1 3.5 %select_reduce_fusion = bf16[5,120,120]{2,1,0:T(8,128)(2,1)S(1)} fusion(f32[5,120,8]{2,1,0:T(8,128)S(1)} %copy.44, s32[5,120,8]{2,1,0:T(8,128)S(1)} %copy.43), kind=kLoop, calls=%fused_computation.12 | loop fusion | flops 1656000 | bytes 182400 | tf_op jit(solution)/shard_map/reduce_sum | solution.py:11
  13.1 0.9 pad_maximum_fusion
  14.0 4.2 %all-to-all-start.1 = ((bf16[4,30,5,512]{3,1,2,0:T(8,128)(2,1)}), bf16[4,30,5,512]{3,1,2,0:T(8,128)(2,1)S(1)}, u32[]{:S(2)}, u32[]{:S(2)}) async-start(bf16[4,30,5,512]{3,1,2,0:T(8,128)(2,1)} %pad_maximum_fusion), calls=%async_computation.1 | async-start | bytes 1310720 | tf_op jit(solution)/shard_map/all_to_all | solution.py:42
  18.5 8.3 %all-to-all-done.1 = bf16[4,30,5,512]{3,1,2,0:T(8,128)(2,1)S(1)} async-done(((bf16[4,30,5,512]{3,1,2,0:T(8,128)(2,1)}), bf16[4,30,5,512]{3,1,2,0:T(8,128)(2,1)S(1)}, u32[]{:S(2)}, u32[]{:S(2)}) %all-to-all-start.1) | async-done | bytes 614432 | tf_op jit(solution)/shard_map/all_to_all | solution.py:42
  27.7 2.7 %gather_fusion = bf16[72,30,5,128]{3,1,2,0:T(8,128)(2,1)} fusion(bf16[30,5,16,128]{3,0,2,1:T(8,128)(2,1)S(1)} %copy.48, s32[1024]{0:T(1024)S(1)} %pad_clamp_fusion), kind=kCustom, calls=%fused_computation | custom fusion | bytes 5529888 | tf_op jit(solution)/shard_map/gather | solution.py:15
  30.5 2.9 %copy.49 = bf16[72,30,5,128]{3,0,2,1:T(8,128)(2,1)S(1)} copy(bf16[72,30,5,128]{3,1,2,0:T(8,128)(2,1)} %gather_fusion) | data formatting | bytes 5529600 | tf_op jit(solution)/shard_map/gather | solution.py:15
  33.4 5.4 %fusion.8 = f32[30,18,128]{2,0,1:T(8,128)S(1)} fusion(bf16[5,18,4,128,128]{4,3,2,1,0:T(8,128)(2,1)} %bitcast.95, bf16[30,5,18,4,128]{4,3,2,1,0:T(4,128)(2,1)S(1)} %bitcast.85), kind=kOutput, calls=%fused_computation.18 | convolution fusion | flops 353894400 | bytes 14837760 | tf_op jit(solution)/shard_map/mkcnd,kcnde->mce/dot_general | solution.py:16
  39.0 1.2 scatter_custom_fusion
  40.9 14.8 %all-to-all-start.2 = ((bf16[30,64,8]{0,2,1:T(8,128)(2,1)}), bf16[30,64,8]{0,2,1:T(8,128)(2,1)S(1)}, u32[]{:S(2)}, u32[]{:S(2)}) async-start(bf16[30,64,8]{0,2,1:T(8,128)(2,1)} %convert_bitcast_fusion.5), calls=%async_computation.2 | async-start | bytes 262144 | tf_op jit(solution)/shard_map/all_to_all | solution.py:32
  56.1 10.0 %all-to-all-done.2 = bf16[30,64,8]{0,2,1:T(8,128)(2,1)S(1)} async-done(((bf16[30,64,8]{0,2,1:T(8,128)(2,1)}), bf16[30,64,8]{0,2,1:T(8,128)(2,1)S(1)}, u32[]{:S(2)}, u32[]{:S(2)}) %all-to-all-start.2) | async-done | bytes 30752 | tf_op jit(solution)/shard_map/all_to_all | solution.py:32
  66.0 3.7 %scatter_custom_fusion.1 = f32[30,2048]{0,1:T(8,128)S(1)} fusion(f32[30,2048]{0,1:T(8,128)S(1)} %bitcast.84, s32[512]{0:T(512)S(1)} %compare_select_fusion, bf16[30,64,8]{0,2,1:T(8,128)(2,1)S(1)} %all-to-all-done.2), kind=kCustom, calls=%fused_computation.25 | custom fusion | flops 30720 | bytes 376832 | tf_op jit(solution)/shard_map/scatter-add | solution.py:55
  70.0 7.2 %all_to_all.66 = bf16[30,4,512]{2,0,1:T(8,128)(2,1)S(1)} all-to-all(bf16[30,4,512]{2,0,1:T(8,128)(2,1)S(1)} %copy.56), channel_id=1, replica_groups=mesh['space'=64,'mode'=4] {'mode'}, dimensions={1} | all-to-all | bytes 245760 | tf_op jit(solution)/shard_map/all_to_all | solution.py:37
  77.9 11.7 %all_to_all.67 = bf16[4,30,5,512]{3,1,2,0:T(8,128)(2,1)S(1)} all-to-all(bf16[4,30,5,512]{3,1,2,0:T(8,128)(2,1)S(1)} %pad_maximum_fusion.1), channel_id=1, replica_groups=mesh['space'=64,'mode'=4] {'mode'}, dimensions={0} | all-to-all | bytes 1228800 | tf_op jit(solution)/shard_map/all_to_all | solution.py:42
  90.5 2.7 %gather_fusion.1 = bf16[72,30,5,128]{3,1,2,0:T(8,128)(2,1)} fusion(bf16[30,5,16,128]{3,0,2,1:T(8,128)(2,1)S(1)} %copy.58, s32[1024]{0:T(1024)S(1)} %pad_clamp_fusion), kind=kCustom, calls=%fused_computation.1 | custom fusion | bytes 5529888 | tf_op jit(solution)/shard_map/gather | solution.py:15
  93.2 2.9 %copy.59 = bf16[72,30,5,128]{3,0,2,1:T(8,128)(2,1)S(1)} copy(bf16[72,30,5,128]{3,1,2,0:T(8,128)(2,1)} %gather_fusion.1) | data formatting | bytes 5529600 | tf_op jit(solution)/shard_map/gather | solution.py:15
  96.1 5.4 %fusion.13 = f32[30,18,128]{2,0,1:T(8,128)S(1)} fusion(bf16[5,18,4,128,128]{4,3,2,1,0:T(8,128)(2,1)} %bitcast.96, bf16[30,5,18,4,128]{4,3,2,1,0:T(4,128)(2,1)S(1)} %bitcast.86), kind=kOutput, calls=%fused_computation.19 | convolution fusion | flops 353894400 | bytes 14837760 | tf_op jit(solution)/shard_map/mkcnd,kcnde->mce/dot_general | solution.py:16
  101.7 1.2 scatter_custom_fusion.2
  103.6 6.9 %all-to-all-start.5 = ((bf16[30,64,8]{0,2,1:T(8,128)(2,1)}), bf16[30,64,8]{0,2,1:T(8,128)(2,1)S(1)}, u32[]{:S(2)}, u32[]{:S(2)}) async-start(bf16[30,64,8]{0,2,1:T(8,128)(2,1)} %convert_bitcast_fusion.4), calls=%async_computation.5 | async-start | bytes 262144 | tf_op jit(solution)/shard_map/all_to_all | solution.py:32
  110.5 0.9 copy.66
  111.8 9.1 %all-to-all-done.5 = bf16[30,64,8]{0,2,1:T(8,128)(2,1)S(1)} async-done(((bf16[30,64,8]{0,2,1:T(8,128)(2,1)}), bf16[30,64,8]{0,2,1:T(8,128)(2,1)S(1)}, u32[]{:S(2)}, u32[]{:S(2)}) %all-to-all-start.5) | async-done | bytes 30752 | tf_op jit(solution)/shard_map/all_to_all | solution.py:32
  120.9 3.7 %scatter_custom_fusion.3 = f32[30,2048]{0,1:T(8,128)S(1)} fusion(f32[30,2048]{0,1:T(8,128)S(1)} %bitcast.83, s32[512]{0:T(512)S(1)} %compare_select_fusion, bf16[30,64,8]{0,2,1:T(8,128)(2,1)S(1)} %all-to-all-done.5), kind=kCustom, calls=%fused_computation.23 | custom fusion | flops 30720 | bytes 376832 | tf_op jit(solution)/shard_map/scatter-add | solution.py:55
  124.7 0.9 copy.67
  (48 shorter events, 8.3 us)
Async XLA Ops:
  2.3 10.3 %all-to-all-start = ((bf16[30,4,512]{2,0,1:T(8,128)(2,1)}), bf16[30,4,512]{2,0,1:T(8,128)(2,1)S(1)}, u32[]{:S(2)}, u32[]{:S(2)}) async-start(bf16[30,4,512]{2,0,1:T(8,128)(2,1)} %copy.45), calls=%async_computation | async-start | bytes 262144 | tf_op jit(solution)/shard_map/all_to_all | solution.py:37
  9.1 9.2 %copy-start = (s32[18,4]{0,1:T(4,128)S(1)}, s32[18,4]{0,1:T(4,128)}, u32[]{:S(2)}) copy-start(s32[18,4]{0,1:T(4,128)} %param.9) | copy-start | bytes 868
  9.1 9.4 %copy-start.2 = (s32[256]{0:T(256)S(1)}, s32[256]{0:T(256)}, u32[]{:S(2)}) copy-start(s32[256]{0:T(256)} %param.10) | copy-start | bytes 3076
  14.0 12.8 %all-to-all-start.1 = ((bf16[4,30,5,512]{3,1,2,0:T(8,128)(2,1)}), bf16[4,30,5,512]{3,1,2,0:T(8,128)(2,1)S(1)}, u32[]{:S(2)}, u32[]{:S(2)}) async-start(bf16[4,30,5,512]{3,1,2,0:T(8,128)(2,1)} %pad_maximum_fusion), calls=%async_computation.1 | async-start | bytes 1310720 | tf_op jit(solution)/shard_map/all_to_all | solution.py:42
  33.4 22.3 %copy-start.1 = (s32[512]{0:T(512)S(1)}, s32[512]{0:T(512)}, u32[]{:S(2)}) copy-start(s32[512]{0:T(512)} %param.11) | copy-start | bytes 6148
  40.9 25.2 %all-to-all-start.2 = ((bf16[30,64,8]{0,2,1:T(8,128)(2,1)}), bf16[30,64,8]{0,2,1:T(8,128)(2,1)S(1)}, u32[]{:S(2)}, u32[]{:S(2)}) async-start(bf16[30,64,8]{0,2,1:T(8,128)(2,1)} %convert_bitcast_fusion.5), calls=%async_computation.2 | async-start | bytes 262144 | tf_op jit(solution)/shard_map/all_to_all | solution.py:32
  103.6 17.3 %all-to-all-start.5 = ((bf16[30,64,8]{0,2,1:T(8,128)(2,1)}), bf16[30,64,8]{0,2,1:T(8,128)(2,1)S(1)}, u32[]{:S(2)}, u32[]{:S(2)}) async-start(bf16[30,64,8]{0,2,1:T(8,128)(2,1)} %convert_bitcast_fusion.4), calls=%async_computation.5 | async-start | bytes 262144 | tf_op jit(solution)/shard_map/all_to_all | solution.py:32
